TPU v7x, 128 devices: a whole 4x4x4 slice. The times are simulated.
128 devices in a mesh: expert: 16 (over y, x_lo, core), tensor: 8 (over x_hi, z).
Axes of the slice: x: 4 (x_hi: 2, x_lo: 2; x = x_hi * 2 + x_lo), y: 4, z: 4, core: 2. Of those that a mesh axis runs over, the one named last changes fastest.
Arguments:
- tokens: bfloat16 [4096, 7168], P(('expert', 'tensor')), may hold values from -6 to 6
- expert_ids: int32 [4096, 2], P('expert'), may hold values from 0 to 2, all different within a row
- gate_scores: int32 [4096, 2], P('expert'), may hold values from 1 to 64
- gate_weight: bfloat16 [3, 7168, 2048], P(None, ('expert', 'tensor')), may hold values from -0.0625 to 0.0625
- up_weight: bfloat16 [3, 7168, 2048], P(None, ('expert', 'tensor')), may hold values from -0.0625 to 0.0625
- down_weight: bfloat16 [3, 7168, 2048], P(None, ('expert', 'tensor')), may hold values from -0.1875 to 0.1875
Outputs:
- mixed: bfloat16 [4096, 7168], P(('expert', 'tensor'))
Inputs may be any that keep to these rules, and one draw needn't show every extreme that they name: `expert_ids`: each row names 2 different experts.
All inputs are finite; a program needn't handle non-finite values.
Results may differ from a plain program's by a relative error of at most 0.015.
Values may be sent and summed in bfloat16 or wider, within the bound.
A program may use at most 128 MiB of HBM per device.

v0:
```python
import jax
import jax.numpy as jnp
from jax import lax
from jax.sharding import PartitionSpec as P


def activate(gate_sum, up_sum, weight_col):
    return (jax.nn.silu(gate_sum) * up_sum * weight_col).astype(jnp.bfloat16)


def local(tokens, expert_ids, gate_scores, gate_weight, up_weight, down_weight):
    gathered = lax.all_gather(tokens, "tensor", axis=0, tiled=True)
    experts = gate_weight.shape[0]
    scores = gate_scores.astype(jnp.float32)
    score_sum = jnp.sum(scores, axis=1, keepdims=True)
    labels = jnp.arange(experts, dtype=jnp.int32)
    picked = (expert_ids[:, :, None] == labels[None, None, :]).astype(jnp.float32)
    combine = jnp.sum(scores[:, :, None] * picked, axis=1) / score_sum
    served_gate, served_up, served_down = (
        lax.all_to_all(gate_weight, "tensor", split_axis=2, concat_axis=1, tiled=True),
        lax.all_to_all(up_weight, "tensor", split_axis=2, concat_axis=1, tiled=True),
        lax.all_to_all(down_weight, "tensor", split_axis=2, concat_axis=1, tiled=True),
    )
    hiddens = []
    full_gate, full_up = (
        lax.all_gather(served_gate, "expert", axis=1, tiled=True),
        lax.all_gather(served_up, "expert", axis=1, tiled=True),
    )
    for which in range(experts):
        gate_sum = jnp.dot(gathered, full_gate[which], preferred_element_type=jnp.float32)
        up_sum = jnp.dot(gathered, full_up[which], preferred_element_type=jnp.float32)
        hiddens.append(activate(gate_sum, up_sum, combine[:, which : which + 1]))
    stacked = jnp.stack(hiddens)
    partial_sum = jnp.einsum(
        "etf,edf->td",
        stacked,
        lax.all_gather(served_down, "expert", axis=1, tiled=True),
        preferred_element_type=jnp.float32,
    )
    output_rows = lax.psum_scatter(
        partial_sum.astype(jnp.bfloat16), "tensor", scatter_dimension=0, tiled=True
    )
    return output_rows


def solution(mesh):
    return jax.shard_map(
        local,
        mesh=mesh,
        in_specs=(
            P(("expert", "tensor"), None),
            P("expert", None),
            P("expert", None),
            P(None, ("expert", "tensor"), None),
            P(None, ("expert", "tensor"), None),
            P(None, ("expert", "tensor"), None),
        ),
        out_specs=P(("expert", "tensor"), None),
        check_vma=False,
    )
```

profile of v0, /device:TPU:0, one launch (start us, length us, event | category | flops | bytes accessed | tf_op | source)
XLA Modules:
  0.0 393.2 jit_solution(62899333029683740)
XLA Ops:
  6.5 0.7 all-gather.5.cloned.1.call-update
  7.3 0.0 all-gather.7.cloned.1.call-start
  7.3 2.8 copy.28
  10.1 2.7 reshape.8
  12.8 25.9 %all_to_all.54 = bf16[8,2,21504]{2,1,0:T(2,128)(2,1)S(1)} all-to-all(bf16[8,2,21504]{2,1,0:T(2,128)(2,1)S(1)} %reshape.8), channel_id=1, replica_groups=mesh['expert'=16,'tensor'=8] {'tensor'}, dimensions={0} | all-to-all | bytes 1376256 | tf_op jit(solution)/shard_map/all_to_all | solution.py:20
  38.8 3.0 reshape.9
  41.8 2.1 copy.37
  44.0 0.0 all-gather.9.cloned.1.call-start
  44.0 1.4 copy.31
  45.4 2.7 reshape.6
  48.1 20.4 %all_to_all.55 = bf16[8,2,21504]{2,1,0:T(2,128)(2,1)S(1)} all-to-all(bf16[8,2,21504]{2,1,0:T(2,128)(2,1)S(1)} %reshape.6), channel_id=1, replica_groups=mesh['expert'=16,'tensor'=8] {'tensor'}, dimensions={0} | all-to-all | bytes 1376256 | tf_op jit(solution)/shard_map/all_to_all | solution.py:21
  68.5 3.0 reshape.7
  71.5 2.2 copy.39
  73.7 0.0 all-gather.11.cloned.1.call-start
  73.8 1.4 copy.34
  75.1 2.7 reshape.4
  77.9 14.4 %all_to_all.56 = bf16[8,2,21504]{2,1,0:T(2,128)(2,1)S(1)} all-to-all(bf16[8,2,21504]{2,1,0:T(2,128)(2,1)S(1)} %reshape.4), channel_id=1, replica_groups=mesh['expert'=16,'tensor'=8] {'tensor'}, dimensions={0} | all-to-all | bytes 1376256 | tf_op jit(solution)/shard_map/all_to_all | solution.py:22
  92.2 3.0 reshape.5
  95.2 2.2 copy.35
  97.4 0.2 reduce-scatter.2.cloned.1.call-start
  97.7 0.0 all-gather.5.cloned.1.call-done
  97.8 58.9 %all-gather.7.cloned.1.call-done = bf16[3,7168,256]{2,1,0:T(8,128)(2,1)} async-done(((bf16[3,448,256]{2,1,0:T(8,128)(2,1)}), bf16[3,7168,256]{2,1,0:T(8,128)(2,1)}) %all-gather.7.cloned.1.call-update) | async-done | bytes 11010064 | tf_op jit(solution)/shard_map/all_gather | solution.py:26
  156.7 4.4 %fusion.2 = f32[256,256]{1,0:T(8,128)S(1)} fusion(bf16[256,7168]{1,0:T(8,128)(2,1)} %all-gather.5.cloned.1.call-done, bf16[3,7168,256]{2,1,0:T(8,128)(2,1)} %all-gather.7.cloned.1.call-done), kind=kOutput, calls=%fused_computation.5 | convolution fusion | flops 939524096 | bytes 7602176 | tf_op jit(solution)/shard_map/dot_general | solution.py:30
  161.1 3.2 fusion.4
  164.3 3.2 fusion.6
  167.6 56.2 %all-gather.9.cloned.1.call-done = bf16[3,7168,256]{2,1,0:T(8,128)(2,1)} async-done(((bf16[3,448,256]{2,1,0:T(8,128)(2,1)}), bf16[3,7168,256]{2,1,0:T(8,128)(2,1)}) %all-gather.9.cloned.1.call-update) | async-done | bytes 11010064 | tf_op jit(solution)/shard_map/all_gather | solution.py:27
  223.8 4.4 %fusion.18 = bf16[1,256,256]{2,1,0:T(8,128)(2,1)S(1)} fusion(bf16[256,7168]{1,0:T(8,128)(2,1)} %all-gather.5.cloned.1.call-done, bf16[3,7168,256]{2,1,0:T(8,128)(2,1)} %all-gather.9.cloned.1.call-done, f32[256,256]{1,0:T(8,128)S(1)} %fusion.2, f32[256]{0:T(256)S(1)} %bitcast.93), kind=kOutput, calls=%fused_computation.25 | convolution fusion | flops 939982848 | bytes 7734272 | tf_op jit(solution)/shard_map/dot_general | solution.py:31
  228.2 3.2 fusion.17
  231.4 3.2 fusion.16
  234.6 56.2 %all-gather.11.cloned.1.call-done = bf16[3,7168,256]{2,1,0:T(8,128)(2,1)} async-done(((bf16[3,448,256]{2,1,0:T(8,128)(2,1)}), bf16[3,7168,256]{2,1,0:T(8,128)(2,1)}) %all-gather.11.cloned.1.call-update) | async-done | bytes 11010064 | tf_op jit(solution)/shard_map/all_gather | solution.py:37
  290.8 12.7 %fusion = bf16[256,7168]{1,0:T(8,128)(2,1)} fusion(bf16[3,7168,256]{2,1,0:T(8,128)(2,1)} %all-gather.11.cloned.1.call-done, bf16[1,256,256]{2,1,0:T(8,128)(2,1)S(1)} %fusion.18, bf16[1,256,256]{2,1,0:T(8,128)(2,1)S(1)} %fusion.17, bf16[1,256,256]{2,1,0:T(8,128)(2,1)S(1)} %fusion.16), kind=kOutput, calls=%fused_computation.1 | convolution fusion | flops 2820800512 | bytes 15073280 | tf_op jit(solution)/shard_map/etf,edf->td/dot_general | solution.py:34
  303.5 83.2 %reduce-scatter.2.cloned.1.call-done = bf16[32,7168]{1,0:T(8,128)(2,1)} async-done(((bf16[256,7168]{1,0:T(8,128)(2,1)}), bf16[32,7168]{1,0:T(8,128)(2,1)}) %reduce-scatter.2.cloned.1.call-update) | async-done | bytes 458768 | tf_op jit(solution)/shard_map/reduce_scatter | solution.py:40
  (22 shorter events, 0.2 us)
Async XLA Ops:
  6.5 91.2 %all-gather.5.cloned.1.call-start = ((), (), s32[]{:S(2)}) async-start(), calls=%async_computation.4 | async-start | bytes 4128768 | tf_op jit(solution)/shard_map/all_gather | solution.py:12
  7.3 149.4 %all-gather.7.cloned.1.call-start = ((), (), s32[]{:S(2)}) async-start(), calls=%async_computation.5 | async-start | bytes 11698176 | tf_op jit(solution)/shard_map/all_gather | solution.py:26
  38.8 5.2 %copy-start = (bf16[3,56,2048]{2,1,0:T(8,128)(2,1)S(1)}, bf16[3,56,2048]{2,1,0:T(8,128)(2,1)}, u32[]{:S(2)}) copy-start(bf16[3,56,2048]{2,1,0:T(8,128)(2,1)} %param.10) | copy-start | bytes 2064388
  44.0 179.8 %all-gather.9.cloned.1.call-start = ((), (), s32[]{:S(2)}) async-start(), calls=%async_computation.6 | async-start | bytes 11698176 | tf_op jit(solution)/shard_map/all_gather | solution.py:27
  68.5 5.3 %copy-start.1 = (bf16[3,56,2048]{2,1,0:T(8,128)(2,1)S(1)}, bf16[3,56,2048]{2,1,0:T(8,128)(2,1)}, u32[]{:S(2)}) copy-start(bf16[3,56,2048]{2,1,0:T(8,128)(2,1)} %param.11) | copy-start | bytes 2064388
  73.7 217.1 %all-gather.11.cloned.1.call-start = ((), (), s32[]{:S(2)}) async-start(), calls=%async_computation.7 | async-start | bytes 11698176 | tf_op jit(solution)/shard_map/all_gather | solution.py:37
  77.8 19.8 %copy-start.2 = (s32[256,2]{0,1:T(2,128)S(1)}, s32[256,2]{0,1:T(2,128)}, u32[]{:S(2)}) copy-start(s32[256,2]{0,1:T(2,128)} %param.8) | copy-start | bytes 6148
  77.9 19.8 %copy-start.3 = (s32[256,2]{0,1:T(2,128)S(1)}, s32[256,2]{0,1:T(2,128)}, u32[]{:S(2)}) copy-start(s32[256,2]{0,1:T(2,128)} %param.7) | copy-start | bytes 6148
  97.4 289.3 %reduce-scatter.2.cloned.1.call-start = ((), (), s32[]{:S(2)}) async-start(), calls=%async_computation.8 | async-start | bytes 4128768 | tf_op jit(solution)/shard_map/reduce_scatter | solution.py:40
  156.7 4.4 %copy-start.4 = (bf16[256,7168]{1,0:T(8,128)(2,1)S(1)}, bf16[256,7168]{1,0:T(8,128)(2,1)}, u32[]{:S(2)}) copy-start(bf16[256,7168]{1,0:T(8,128)(2,1)} %all-gather.5.cloned.1.call-done) | copy-start | bytes 11010052
  223.8 4.4 %copy-start.5 = (bf16[256,7168]{1,0:T(8,128)(2,1)S(1)}, bf16[256,7168]{1,0:T(8,128)(2,1)}, u32[]{:S(2)}) copy-start(bf16[256,7168]{1,0:T(8,128)(2,1)} %all-gather.5.cloned.1.call-done) | copy-start | bytes 11010052
Sparse Core Ops, SparseCore 0:
  9.7 83.9 all-gather.4
  95.3 61.3 all-gather.6
  158.4 65.3 all-gather.8
  225.3 65.3 all-gather.10
  303.6 83.0 reduce-scatter.1
where the time goes:
time: 394 us; the launch traced here: 393 us
  waiting for transfers between devices  255 us (65%)
  blocking collectives  60.7 us (15%)
  matrix products  34.3 us (9%)
  local copies, waits for them, and re-layouts  29.2 us (7%)
  between operations  13.3 us (3%)
    reduce_scatter x1, waiting for transfers between devices, local(): lax.psum_scatter(partial_sum.astype(jnp.bfloat16), 'tensor', scatter_dime...  83.2 us
    all_gather x1, waiting for transfers between devices, local(): lax.all_gather(served_gate, 'expert', axis=1, tiled=True)  58.9 us
    all_gather x1, waiting for transfers between devices, local(): lax.all_gather(served_up, 'expert', axis=1, tiled=True)  56.2 us
    all_gather x1, waiting for transfers between devices, local(): lax.all_gather(served_down, 'expert', axis=1, tiled=True)  56.2 us
    all_to_all x1, blocking collectives, local(): lax.all_to_all(gate_weight, 'tensor', split_axis=2, concat_axis=1, tiled=...  25.9 us
    unnamed x21, local copies, waits for them, and re-layouts  22.7 us
    all_to_all x1, blocking collectives, local(): lax.all_to_all(up_weight, 'tensor', split_axis=2, concat_axis=1, tiled=True)  20.4 us
    all_to_all x1, blocking collectives, local(): lax.all_to_all(down_weight, 'tensor', split_axis=2, concat_axis=1, tiled=...  14.4 us
  transfers between devices with their start and end apart: 5, of which 4 were waited for; matrix products, arithmetic and copies ran while one was open for 13% of the time, Pallas kernels for 0%

commit v1 on v0

--- a/solution.py
+++ b/solution.py
@@ -17,7 +17,12 @@
     picked = (expert_ids[:, :, None] == labels[None, None, :]).astype(jnp.float32)
     combine = jnp.sum(scores[:, :, None] * picked, axis=1) / score_sum
     served_gate, served_up, served_down = (
-        lax.all_to_all(gate_weight, "tensor", split_axis=2, concat_axis=1, tiled=True),
+        jnp.concatenate(
+            lax.all_to_all(
+                jnp.stack(jnp.split(gate_weight, lax.axis_size("tensor"), axis=2)), "tensor", 0, 0
+            ),
+            axis=1,
+        ),
         lax.all_to_all(up_weight, "tensor", split_axis=2, concat_axis=1, tiled=True),
         lax.all_to_all(down_weight, "tensor", split_axis=2, concat_axis=1, tiled=True),
     )

time: 394 us -> 393 us (level)
    unnamed x21 -> x25, local copies, waits for them, and re-layouts: 22.7 us -> 20.4 us
where the time goes in v1:
time: 393 us
  waiting for transfers between devices  257 us (65%)
  blocking collectives  59.6 us (15%)
  matrix products  35.9 us (9%)
  local copies, waits for them, and re-layouts  26.6 us (7%)
  between operations  13.3 us (3%)
    reduce_scatter x1, waiting for transfers between devices, local(): lax.psum_scatter(partial_sum.astype(jnp.bfloat16), 'tensor', scatter_dime...  83.4 us
    all_gather x1, waiting for transfers between devices, local(): lax.all_gather(served_gate, 'expert', axis=1, tiled=True)  61.9 us
    all_gather x1, waiting for transfers between devices, local(): lax.all_gather(served_up, 'expert', axis=1, tiled=True)  56.2 us
    all_gather x1, waiting for transfers between devices, local(): lax.all_gather(served_down, 'expert', axis=1, tiled=True)  54.7 us
    all_to_all x1, blocking collectives, local(): lax.all_to_all(jnp.stack(jnp.split(gate_weight, lax.axis_size('tensor'),...  25.9 us
    unnamed x25, local copies, waits for them, and re-layouts  20.4 us
    all_to_all x1, blocking collectives, local(): lax.all_to_all(up_weight, 'tensor', split_axis=2, concat_axis=1, tiled=True)  19.5 us
    all_to_all x1, blocking collectives, local(): lax.all_to_all(down_weight, 'tensor', split_axis=2, concat_axis=1, tiled=...  14.2 us
  transfers between devices with their start and end apart: 5, of which 4 were waited for; matrix products, arithmetic and copies ran while one was open for 13% of the time, Pallas kernels for 0%

profile of v1, /device:TPU:0, one launch (start us, length us, event | category | flops | bytes accessed | tf_op | source)
XLA Modules:
  0.0 392.8 jit_solution(14080308929781784453)
XLA Ops:
  6.5 0.7 all-gather.7.cloned.1.call-update
  7.3 0.9 bitcast_dynamic-update-slice_fusion.7
  8.2 0.9 bitcast_dynamic-update-slice_fusion.6
  9.1 0.9 bitcast_dynamic-update-slice_fusion.5
  10.0 0.9 bitcast_dynamic-update-slice_fusion.4
  10.9 0.9 bitcast_dynamic-update-slice_fusion.3
  11.8 0.9 bitcast_dynamic-update-slice_fusion.2
  12.7 0.9 bitcast_dynamic-update-slice_fusion.1
  13.6 0.9 bitcast_dynamic-update-slice_fusion
  14.5 25.9 %all_to_all.41 = bf16[8,3,56,256]{3,2,1,0:T(8,128)(2,1)S(1)} all-to-all(bf16[8,3,56,256]{3,2,1,0:T(8,128)(2,1)S(1)} %bitcast_dynamic-update-slice_fusion), channel_id=1, replica_groups=mesh['expert'=16,'tensor'=8] {'tensor'}, dimensions={0} | all-to-all | bytes 1376256 | tf_op jit(solution)/shard_map/all_to_all | solution.py:21
  40.4 0.9 copy.41
  41.4 1.4 copy.42
  42.7 2.7 reshape.14
  45.4 19.5 %all_to_all.42 = bf16[8,2,21504]{2,1,0:T(2,128)(2,1)S(1)} all-to-all(bf16[8,2,21504]{2,1,0:T(2,128)(2,1)S(1)} %reshape.14), channel_id=1, replica_groups=mesh['expert'=16,'tensor'=8] {'tensor'}, dimensions={0} | all-to-all | bytes 1376256 | tf_op jit(solution)/shard_map/all_to_all | solution.py:26
  64.9 3.0 reshape.15
  67.9 2.2 copy.56
  70.2 1.4 copy.48
  71.6 2.7 reshape.12
  74.3 14.2 %all_to_all.43 = bf16[8,2,21504]{2,1,0:T(2,128)(2,1)S(1)} all-to-all(bf16[8,2,21504]{2,1,0:T(2,128)(2,1)S(1)} %reshape.12), channel_id=1, replica_groups=mesh['expert'=16,'tensor'=8] {'tensor'}, dimensions={0} | all-to-all | bytes 1376256 | tf_op jit(solution)/shard_map/all_to_all | solution.py:27
  88.5 3.0 reshape.13
  91.5 2.2 copy.49
  94.0 61.9 %all-gather.5.cloned.1.call-done = bf16[3,7168,256]{2,1,0:T(8,128)(2,1)} async-done(((bf16[3,448,256]{2,1,0:T(8,128)(2,1)}), bf16[3,7168,256]{2,1,0:T(8,128)(2,1)}) %all-gather.5.cloned.1.call-update) | async-done | bytes 11010064 | tf_op jit(solution)/shard_map/all_gather | solution.py:31
  156.0 4.5 %fusion.9 = f32[256,256]{0,1:T(8,128)S(1)} fusion(bf16[256,7168]{1,0:T(8,128)(2,1)} %all-gather.7.cloned.1.call-done, bf16[3,7168,256]{2,1,0:T(8,128)(2,1)} %all-gather.5.cloned.1.call-done), kind=kOutput, calls=%fused_computation.16 | convolution fusion | flops 939524096 | bytes 7602176 | tf_op jit(solution)/shard_map/dot_general | solution.py:35
  160.4 3.2 fusion.8
  163.6 3.2 fusion.7
  166.8 56.2 %all-gather.9.cloned.1.call-done = bf16[3,7168,256]{2,1,0:T(8,128)(2,1)} async-done(((bf16[3,448,256]{2,1,0:T(8,128)(2,1)}), bf16[3,7168,256]{2,1,0:T(8,128)(2,1)}) %all-gather.9.cloned.1.call-update) | async-done | bytes 11010064 | tf_op jit(solution)/shard_map/all_gather | solution.py:32
  223.1 4.8 %fusion.21 = bf16[1,256,256]{1,2,0:T(8,128)(2,1)S(1)} fusion(bf16[256,7168]{1,0:T(8,128)(2,1)} %all-gather.7.cloned.1.call-done, bf16[3,7168,256]{2,1,0:T(8,128)(2,1)} %all-gather.9.cloned.1.call-done, f32[256,256]{0,1:T(8,128)S(1)} %fusion.9, f32[256]{0:T(256)S(1)} %bitcast.115), kind=kOutput, calls=%fused_computation.28 | convolution fusion | flops 939982848 | bytes 7734272 | tf_op jit(solution)/shard_map/dot_general | solution.py:36
  227.9 3.7 fusion.20
  231.6 3.7 fusion.19
  235.4 54.7 %all-gather.11.cloned.1.call-done = bf16[3,7168,256]{2,1,0:T(8,128)(2,1)} async-done(((bf16[3,448,256]{2,1,0:T(8,128)(2,1)}), bf16[3,7168,256]{2,1,0:T(8,128)(2,1)}) %all-gather.11.cloned.1.call-update) | async-done | bytes 11010064 | tf_op jit(solution)/shard_map/all_gather | solution.py:42
  290.0 12.8 %fusion = bf16[256,7168]{1,0:T(8,128)(2,1)} fusion(bf16[3,7168,256]{2,1,0:T(8,128)(2,1)} %all-gather.11.cloned.1.call-done, bf16[1,256,256]{1,2,0:T(8,128)(2,1)S(1)} %fusion.21, bf16[1,256,256]{1,2,0:T(8,128)(2,1)S(1)} %fusion.20, bf16[1,256,256]{1,2,0:T(8,128)(2,1)S(1)} %fusion.19), kind=kOutput, calls=%fused_computation.1 | convolution fusion | flops 2820800512 | bytes 15073280 | tf_op jit(solution)/shard_map/etf,edf->td/dot_general | solution.py:39
  302.9 83.4 %reduce-scatter.2.cloned.1.call-done = bf16[32,7168]{1,0:T(8,128)(2,1)} async-done(((bf16[256,7168]{1,0:T(8,128)(2,1)}), bf16[32,7168]{1,0:T(8,128)(2,1)}) %reduce-scatter.2.cloned.1.call-update) | async-done | bytes 458768 | tf_op jit(solution)/shard_map/reduce_scatter | solution.py:45
  (27 shorter events, 0.5 us)
Async XLA Ops:
  6.5 34.8 %copy-start = (bf16[3,56,2048]{2,1,0:T(8,128)(2,1)S(1)}, bf16[3,56,2048]{2,1,0:T(8,128)(2,1)}, u32[]{:S(2)}) copy-start(bf16[3,56,2048]{2,1,0:T(8,128)(2,1)} %param.10) | copy-start | bytes 2064388
  6.5 87.5 %all-gather.7.cloned.1.call-start = ((), (), s32[]{:S(2)}) async-start(), calls=%async_computation.5 | async-start | bytes 4128768 | tf_op jit(solution)/shard_map/all_gather | solution.py:12
  7.3 148.7 %all-gather.5.cloned.1.call-start = ((), (), s32[]{:S(2)}) async-start(), calls=%async_computation.4 | async-start | bytes 11698176 | tf_op jit(solution)/shard_map/all_gather | solution.py:31
  41.3 181.8 %all-gather.9.cloned.1.call-start = ((), (), s32[]{:S(2)}) async-start(), calls=%async_computation.6 | async-start | bytes 11698176 | tf_op jit(solution)/shard_map/all_gather | solution.py:32
  64.9 5.3 %copy-start.1 = (bf16[3,56,2048]{2,1,0:T(8,128)(2,1)S(1)}, bf16[3,56,2048]{2,1,0:T(8,128)(2,1)}, u32[]{:S(2)}) copy-start(bf16[3,56,2048]{2,1,0:T(8,128)(2,1)} %param.11) | copy-start | bytes 2064388
  70.1 219.9 %all-gather.11.cloned.1.call-start = ((), (), s32[]{:S(2)}) async-start(), calls=%async_computation.7 | async-start | bytes 11698176 | tf_op jit(solution)/shard_map/all_gather | solution.py:42
  74.3 19.7 %copy-start.2 = (s32[256,2]{0,1:T(2,128)S(1)}, s32[256,2]{0,1:T(2,128)}, u32[]{:S(2)}) copy-start(s32[256,2]{0,1:T(2,128)} %param.8) | copy-start | bytes 6148
  74.3 19.7 %copy-start.3 = (s32[256,2]{0,1:T(2,128)S(1)}, s32[256,2]{0,1:T(2,128)}, u32[]{:S(2)}) copy-start(s32[256,2]{0,1:T(2,128)} %param.7) | copy-start | bytes 6148
  93.7 292.6 %reduce-scatter.2.cloned.1.call-start = ((), (), s32[]{:S(2)}) async-start(), calls=%async_computation.8 | async-start | bytes 4128768 | tf_op jit(solution)/shard_map/reduce_scatter | solution.py:45
  156.0 4.5 %copy-start.4 = (bf16[256,7168]{1,0:T(8,128)(2,1)S(1)}, bf16[256,7168]{1,0:T(8,128)(2,1)}, u32[]{:S(2)}) copy-start(bf16[256,7168]{1,0:T(8,128)(2,1)} %all-gather.7.cloned.1.call-done) | copy-start | bytes 11010052
  223.1 4.8 %copy-start.5 = (bf16[256,7168]{1,0:T(8,128)(2,1)S(1)}, bf16[256,7168]{1,0:T(8,128)(2,1)}, u32[]{:S(2)}) copy-start(bf16[256,7168]{1,0:T(8,128)(2,1)} %all-gather.7.cloned.1.call-done) | copy-start | bytes 11010052
Sparse Core Ops, SparseCore 0:
  9.7 82.5 all-gather.6
  93.9 62.0 all-gather.4
  157.6 65.3 all-gather.8
  224.6 65.3 all-gather.10
  303.0 83.2 reduce-scatter.1
